TPU v7x, 32 devices: a whole 2x2x4 slice. The times are simulated.
32 devices in a mesh: node: 8 (over z, x), feat: 4 (over y, core).
Axes of the slice: x: 2, y: 2, z: 4, core: 2. Of those that a mesh axis runs over, the one named last changes fastest.
Arguments:
- feature_table: bfloat16 [8192, 2048], P('node', 'feat'), may hold values from -6 to 6
- hub_table: bfloat16 [32, 2048], P('node', 'feat'), may hold values from -6 to 6
- first_self: bfloat16 [2048, 2048], P('feat'), may hold values from -0.125 to 0.125
- first_pooled: bfloat16 [2048, 2048], P('feat'), may hold values from -0.125 to 0.125
- second_self: bfloat16 [2048, 256], P('feat'), may hold values from -0.125 to 0.125
- second_pooled: bfloat16 [2048, 256], P('feat'), may hold values from -0.125 to 0.125
- first_lists: int32 [3072, 10], P('node'), may hold values from 0 to 8223, as said below
- first_counts: int32 [3072], P('node'), may hold values from 1 to 10
- second_lists: int32 [2048, 5], P('node'), may hold values from 0 to 3071, as said below
- second_counts: int32 [2048], P('node'), may hold values from 1 to 5
Outputs:
- embedding: bfloat16 [2048, 256], P(('node', 'feat'))
Inputs may be any that keep to these rules, and one draw needn't show every extreme that they name: `first_lists`: an entry below 8192 names a row of feature_table, held by node shard (entry // 1024); an entry v of 8192 or more names hub clip v - 8192, owned by node shard (v - 8192) // 4. Slots at or beyond a clip's count are padding and still hold such entries. Of the 3840 entries of one node shard's rows, padding included, at most 480 name feature rows held by any one node shard; in every draw one node shard is named exactly 480 times by the rows of every node shard. `second_lists`: entries name frontier clips, held by node shard (entry // 384). Of the 1280 entries of one node shard's rows, padding included, exactly 160 name frontier clips of each node shard.
All inputs are finite; a program needn't handle non-finite values.
Results may differ from a plain program's by a relative error of at most 0.0052.
Values may be sent and summed in bfloat16 or wider, within the bound.
A program may use at most 64 MiB of HBM per device.

v0:
```python
import jax
import jax.numpy as jnp
from jax import lax
from jax.sharding import PartitionSpec as P


def count_matrix(local, width):
    columns = jnp.arange(width, dtype=jnp.int32)[None, :]
    total = jnp.zeros((local.shape[0], width), jnp.float32)
    for k in range(local.shape[1]):
        total = total + (local[:, k : k + 1] == columns).astype(jnp.float32)
    return total.astype(jnp.bfloat16)


def body(
    feature_table,
    hub_table,
    first_self,
    first_pooled,
    second_self,
    second_pooled,
    first_lists,
    first_counts,
    second_lists,
    second_counts,
):
    shards = lax.axis_size("node")
    me = lax.axis_index("node")
    rows_here = feature_table.shape[0]
    hubs_here = hub_table.shape[0]
    front_here, fan_one = first_lists.shape
    targets_here, fan_two = second_lists.shape
    total_rows = rows_here * shards
    slots_one = jnp.arange(fan_one, dtype=jnp.int32)[None, :]
    slots_two = jnp.arange(fan_two, dtype=jnp.int32)[None, :]
    lists_one = jnp.where(slots_one < first_counts[:, None], first_lists, -1)
    lists_two = jnp.where(slots_two < second_counts[:, None], second_lists, -1)
    packed = jnp.concatenate([lists_one.reshape(-1), lists_two.reshape(-1), second_counts]).reshape(
        1, -1
    )
    everyone = lax.all_gather(packed, "node", axis=0, tiled=True)
    cut_one = front_here * fan_one
    cut_two = cut_one + targets_here * fan_two
    all_one = everyone[:, :cut_one].reshape(shards * front_here, fan_one)
    all_two = everyone[:, cut_one:cut_two].reshape(shards * targets_here, fan_two)
    all_counts = everyone[:, cut_two:].reshape(shards * targets_here, 1)
    feature_at = all_one - me * rows_here
    hub_at = all_one - total_rows - me * hubs_here
    local_one = jnp.where(
        (feature_at >= 0) & (feature_at < rows_here) & (all_one >= 0),
        feature_at,
        jnp.where((hub_at >= 0) & (hub_at < hubs_here), hub_at + rows_here, -1),
    )
    combined = jnp.concatenate([feature_table, hub_table], axis=0)
    matrix_one = count_matrix(local_one, rows_here + hubs_here)
    sums = jnp.dot(matrix_one, combined, preferred_element_type=jnp.float32)
    sums = lax.psum_scatter(sums.astype(jnp.bfloat16), "node", scatter_dimension=0, tiled=True)
    first_mean = (sums.astype(jnp.float32) / first_counts[:, None].astype(jnp.float32)).astype(
        jnp.bfloat16
    )
    part = jnp.dot(feature_table[:front_here], first_self, preferred_element_type=jnp.float32)
    part = part + jnp.dot(first_mean, first_pooled, preferred_element_type=jnp.float32)
    hidden = jax.nn.relu(
        lax.psum_scatter(part.astype(jnp.bfloat16), "feat", scatter_dimension=1, tiled=True)
    )
    projected = jnp.dot(hidden, second_pooled, preferred_element_type=jnp.float32)
    own = jnp.dot(hidden[:targets_here], second_self, preferred_element_type=jnp.float32)
    local_two = jnp.where(all_two >= 0, all_two - me * front_here, -1)
    matrix_two = count_matrix(local_two, front_here)
    mixed = jnp.dot(
        matrix_two, projected.astype(jnp.bfloat16), preferred_element_type=jnp.float32
    ) / all_counts.astype(jnp.float32)
    here = lax.dynamic_slice_in_dim(mixed, me * targets_here, targets_here, 0)
    mixed = lax.dynamic_update_slice_in_dim(mixed, here + own, me * targets_here, 0)
    mixed = lax.psum_scatter(mixed, ("node", "feat"), scatter_dimension=0, tiled=True)
    scale = lax.rsqrt(jnp.mean(mixed * mixed, axis=1, keepdims=True) + 1e-06)
    return (mixed * scale).astype(jnp.bfloat16)


def solution(mesh):
    return jax.shard_map(
        body,
        mesh=mesh,
        in_specs=(
            P("node", "feat"),
            P("node", "feat"),
            P("feat", None),
            P("feat", None),
            P("feat", None),
            P("feat", None),
            P("node", None),
            P("node"),
            P("node", None),
            P("node"),
        ),
        out_specs=P(("node", "feat"), None),
        check_vma=False,
    )
```

profile of v0, /device:TPU:0, one launch (start us, length us, event | category | flops | bytes accessed | tf_op | source)
XLA Modules:
  0.0 341.4 jit_solution(16329909199386390386)
XLA Ops:
  6.5 0.9 fusion.27
  7.7 0.7 fusion.25
  8.8 0.7 pad_add_fusion
  9.5 32.4 %all-gather.1 = s32[8,1,5376]{2,1,0:T(1,128)S(1)} all-gather(s32[1,1,5376]{2,1,0:T(1,128)S(1)} %reshape.59), channel_id=2, replica_groups=mesh['node'=8,'feat'=4] {'node'}, dimensions={0}, use_global_device_ids=true | all-gather | bytes 193536 | tf_op jit(solution)/shard_map/all_gather | solution.py:41
  42.0 1.8 ge.24
  43.8 2.8 reshape.57
  46.6 2.8 sub.31
  49.4 2.3 and_select_fusion
  51.7 7.9 %slice_reduce_fusion.9 = (s32[3072]{0:T(1024)S(1)}, s32[3072]{0:T(1024)S(1)}, s32[3072]{0:T(1024)S(1)}, s32[3072]{0:T(1024)S(1)}, s32[3072]{0:T(1024)S(1)}, /*in...) fusion(s32[3072,10]{1,0:T(8,128)S(1)} %and_select_fusion), kind=kLoop, calls=%fused_computation.40 | loop fusion | bytes 245760 | tf_op jit(solution)/shard_map/slice | solution.py:11
  59.7 19.4 %fusion.11 = bf16[3072,512]{1,0:T(8,128)(2,1)} fusion(s32[3072]{0:T(1024)S(1)} %get-tuple-element.6, s32[3072]{0:T(1024)S(1)} %get-tuple-element.7, s32[3072]{0:T(1024)S(1)} %get-tuple-element.8, s32[3072]{0:T(1024)S(1)} %get-tuple-element.9, s32[3072]{0:T(1024)S(1)} %get-tuple-element.10, s32[3072]{0:T(1024)S(1)} %get-tuple-element.11, ...), kind=kOutput, calls=%fused_computation.22 | convolution fusion | flops 3332227072 | bytes 4321280 | tf_op jit(solution)/shard_map/dot_general | solution.py:56
  79.1 0.6 copy-done.3
  79.8 3.6 %fusion.22 = f32[384,2048]{1,0:T(8,128)} fusion(bf16[512,2048]{1,0:T(8,128)(2,1)S(1)} %copy-done, bf16[1024,512]{1,0:T(8,128)(2,1)} %param.10), kind=kOutput, calls=%fused_computation.60 | convolution fusion | flops 805306368 | bytes 5636096 | tf_op jit(solution)/shard_map/dot_general | solution.py:61
  83.4 71.1 %reduce-scatter.4.cloned.1.call-done = bf16[384,512]{1,0:T(8,128)(2,1)} async-done(((bf16[3072,512]{1,0:T(8,128)(2,1)}), bf16[384,512]{1,0:T(8,128)(2,1)}) %reduce-scatter.4.cloned.1.call-update) | async-done | bytes 393232 | tf_op jit(solution)/shard_map/reduce_scatter | solution.py:57
  154.5 4.8 %add_convert_fusion.4 = bf16[384,2048]{1,0:T(8,128)(2,1)} fusion(f32[384,2048]{1,0:T(8,128)} %fusion.22, bf16[512,2048]{1,0:T(8,128)(2,1)} %param.13, bf16[384,512]{1,0:T(8,128)(2,1)} %reduce-scatter.4.cloned.1.call-done, f32[384]{0:T(512)S(1)} %convert_element_type.103), kind=kOutput, calls=%fused_computation.23 | convolution fusion | flops 807469056 | bytes 7210496 | tf_op jit(solution)/shard_map/dot_general | solution.py:62
  159.3 0.3 reduce-scatter.8.cloned.1.call-start
  159.7 0.9 select_n.30
  160.6 2.5 slice_reduce_fusion.14
  163.1 23.5 %reduce-scatter.6.cloned.1.call-done = bf16[384,512]{1,0:T(8,128)(2,1)} async-done(((bf16[384,2048]{1,0:T(8,128)(2,1)}), bf16[384,512]{1,0:T(8,128)(2,1)}) %reduce-scatter.6.cloned.1.call-update) | async-done | bytes 393232 | tf_op jit(solution)/shard_map/reduce_scatter | solution.py:64
  186.6 1.0 broadcast_maximum_fusion
  187.7 4.7 %convolution_divide_fusion = f32[2048,256]{1,0:T(8,128)} fusion(s32[2048]{0:T(1024)S(1)} %get-tuple-element.16, s32[2048]{0:T(1024)S(1)} %get-tuple-element.17, s32[2048]{0:T(1024)S(1)} %get-tuple-element.18, s32[2048]{0:T(1024)S(1)} %get-tuple-element.19, s32[2048]{0:T(1024)S(1)} %get-tuple-element.15, bf16[512,256]{1,0:T(8,128)(2,1)S(1)} %copy-done.4, ...), kind=kOutput, calls=%fused_computation.30 | convolution fusion | flops 515932160 | bytes 2801664 | tf_op jit(solution)/shard_map/dot_general | solution.py:70
  192.4 1.9 fusion.17
  194.2 138.1 %reduce-scatter.8.cloned.1.call-done = f32[64,256]{1,0:T(8,128)} async-done(((f32[2048,256]{1,0:T(8,128)}), f32[64,256]{1,0:T(8,128)}) %reduce-scatter.8.cloned.1.call-update) | async-done | bytes 65552 | tf_op jit(solution)/shard_map/reduce_scatter | solution.py:75
  332.4 0.9 multiply_reduce_fusion
  333.3 1.5 multiply_convert_fusion
  (29 shorter events, 0.9 us)
Async XLA Ops:
  6.5 73.2 %copy-start = (bf16[512,2048]{1,0:T(8,128)(2,1)S(1)}, bf16[512,2048]{1,0:T(8,128)(2,1)}, u32[]{:S(2)}) copy-start(bf16[512,2048]{1,0:T(8,128)(2,1)} %param.12) | copy-start | bytes 6291460
  6.5 148.0 %reduce-scatter.4.cloned.1.call-start = ((), (), s32[]{:S(2)}) async-start(), calls=%async_computation.3 | async-start | bytes 3538944 | tf_op jit(solution)/shard_map/reduce_scatter | solution.py:57
  51.7 7.9 %copy-start.2 = (bf16[1024,512]{1,0:T(8,128)(2,1)S(1)}, bf16[1024,512]{1,0:T(8,128)(2,1)}, u32[]{:S(2)}) copy-start(bf16[1024,512]{1,0:T(8,128)(2,1)} %param.10) | copy-start | bytes 3145732
  51.7 7.9 %copy-start.5 = (bf16[4,512]{1,0:T(4,128)(2,1)S(1)}, bf16[4,512]{1,0:T(4,128)(2,1)}, u32[]{:S(2)}) copy-start(bf16[4,512]{1,0:T(4,128)(2,1)} %param.11) | copy-start | bytes 12292
  79.1 0.7 copy-start.3
  79.1 107.5 %reduce-scatter.6.cloned.1.call-start = ((), (), s32[]{:S(2)}) async-start(), calls=%async_computation.4 | async-start | bytes 1966080 | tf_op jit(solution)/shard_map/reduce_scatter | solution.py:64
  159.3 173.0 %reduce-scatter.8.cloned.1.call-start = ((), (), s32[]{:S(2)}) async-start(), calls=%async_computation.5 | async-start | bytes 2162688 | tf_op jit(solution)/shard_map/reduce_scatter | solution.py:75
  160.6 27.1 %copy-start.4 = (bf16[512,256]{1,0:T(8,128)(2,1)S(1)}, bf16[512,256]{1,0:T(8,128)(2,1)}, u32[]{:S(2)}) copy-start(bf16[512,256]{1,0:T(8,128)(2,1)} %param.15) | copy-start | bytes 786436
  187.6 4.7 %copy-start.1 = (bf16[512,256]{1,0:T(8,128)(2,1)S(1)}, bf16[512,256]{1,0:T(8,128)(2,1)}, u32[]{:S(2)}) copy-start(bf16[512,256]{1,0:T(8,128)(2,1)} %param.14) | copy-start | bytes 786436
Sparse Core Ops, SparseCore 0:
  79.2 75.2 reduce-scatter.3
  159.5 27.0 reduce-scatter.5
  194.4 137.9 reduce-scatter.7
where the time goes:
time: 342 us; the launch traced here: 341 us
  waiting for transfers between devices  233 us (68%)
  matrix products  34.4 us (10%)
  blocking collectives  32.4 us (9%)
  local copies, waits for them, and re-layouts  20 us (6%)
  between operations  13.3 us (4%)
  other arithmetic  8.17 us (2%)
    reduce_scatter x1, waiting for transfers between devices, body(): lax.psum_scatter(mixed, ('node', 'feat'), scatter_dimension=0, tiled=True)  138 us
    reduce_scatter x1, waiting for transfers between devices, body(): lax.psum_scatter(sums.astype(jnp.bfloat16), 'node', scatter_dimension=0,...  71.1 us
    all_gather x1, blocking collectives, body(): everyone = lax.all_gather(packed, 'node', axis=0, tiled=True)  32.4 us
    reduce_scatter x1, waiting for transfers between devices, body(): lax.psum_scatter(part.astype(jnp.bfloat16), 'feat', scatter_dimension=1,...  23.5 us
    dot_general x1, matrix products, body(): sums = jnp.dot(matrix_one, combined, preferred_element_type=jnp.float32)  19.4 us
    slice x2, local copies, waits for them, and re-layouts, count_matrix(): total = total + (local[:, k:k + 1] == columns).astype(jnp.float32)  10.4 us
  transfers between devices with their start and end apart: 3, of which 3 were waited for; matrix products, arithmetic and copies ran while one was open for 2% of the time, Pallas kernels for 0%

commit v1 on v0

--- a/solution.py
+++ b/solution.py
@@ -38,7 +38,16 @@
     packed = jnp.concatenate([lists_one.reshape(-1), lists_two.reshape(-1), second_counts]).reshape(
         1, -1
     )
-    everyone = lax.all_gather(packed, "node", axis=0, tiled=True)
+    b_now = lax.axis_size("node")
+    r_now, a_now, e_next = (b_now, lax.axis_index("node"), packed.shape[0])
+    now, back = (packed, 1)
+    while back < r_now:
+        sheets = []
+        for dev in range(r_now):
+            sheets.append((dev, (dev - back) % r_now))
+        now = jnp.concatenate([now, lax.ppermute(now, "node", sheets)], axis=0)
+        back = 2 * back
+    everyone = jnp.roll(now, a_now * e_next, axis=0)
     cut_one = front_here * fan_one
     cut_two = cut_one + targets_here * fan_two
     all_one = everyone[:, :cut_one].reshape(shards * front_here, fan_one)

time: 342 us -> 330 us (0.965)
  blocking collectives: 32.4 us -> 0 us
  waiting for transfers between devices: 233 us -> 245 us
  starting transfers between devices: 0.31 us -> 8.22 us
    all_gather x1 -> x0, blocking collectives: 32.4 us -> none  [body(): everyone = lax.all_gather(packed, 'node', axis=0, tiled=True)]
    ppermute x0 -> x3, waiting for transfers between devices: none -> 10.1 us  [body(): now = jnp.concatenate([now, lax.ppermute(now, 'node', sheets)], axis=0)]
    ppermute x0 -> x3, starting transfers between devices: none -> 7.91 us  [body(): now = jnp.concatenate([now, lax.ppermute(now, 'node', sheets)], axis=0)]
  transfers between devices with their start and end apart: 3 -> 6, of which waited for: 3 -> 6; matrix products, arithmetic and copies ran while one was open for 2% -> 2% of each run, Pallas kernels for 0% -> 0%
where the time goes in v1:
time: 330 us
  waiting for transfers between devices  245 us (74%)
  matrix products  34.4 us (10%)
  local copies, waits for them, and re-layouts  20.2 us (6%)
  between operations  13.3 us (4%)
  other arithmetic  8.45 us (3%)
  starting transfers between devices  8.22 us (2%)
    reduce_scatter x1, waiting for transfers between devices, body(): lax.psum_scatter(mixed, ('node', 'feat'), scatter_dimension=0, tiled=True)  139 us
    reduce_scatter x1, waiting for transfers between devices, body(): lax.psum_scatter(sums.astype(jnp.bfloat16), 'node', scatter_dimension=0,...  73 us
    reduce_scatter x1, waiting for transfers between devices, body(): lax.psum_scatter(part.astype(jnp.bfloat16), 'feat', scatter_dimension=1,...  23.4 us
    dot_general x1, matrix products, body(): sums = jnp.dot(matrix_one, combined, preferred_element_type=jnp.float32)  19.4 us
    slice x2, local copies, waits for them, and re-layouts, count_matrix(): total = total + (local[:, k:k + 1] == columns).astype(jnp.float32)  10.4 us
    ppermute x3, waiting for transfers between devices, body(): now = jnp.concatenate([now, lax.ppermute(now, 'node', sheets)], axis=0)  10.1 us
    ppermute x3, starting transfers between devices, body(): now = jnp.concatenate([now, lax.ppermute(now, 'node', sheets)], axis=0)  7.91 us
  transfers between devices with their start and end apart: 6, of which 6 were waited for; matrix products, arithmetic and copies ran while one was open for 2% of the time, Pallas kernels for 0%

profile of v1, /device:TPU:0, one launch (start us, length us, event | category | flops | bytes accessed | tf_op | source)
XLA Modules:
  0.0 329.8 jit_solution(3982592191175691346)
XLA Ops:
  6.5 0.9 fusion.27
  9.5 6.1 %collective-permute-start = (s32[1,5376]{1,0:T(1,128)S(1)}, s32[1,5376]{1,0:T(1,128)S(1)}, u32[]{:S(2)}, u32[]{:S(2)}) collective-permute-start(s32[1,5376]{1,0:T(1,128)S(1)} %reshape.55), channel_id=1, source_target_pairs={{0,28},{4,0},{8,4},{12,8},{16,12},{20,16},{24,20},{28,24},{1,29},{... | collective-permute-start | bytes 64520 | tf_op jit(solution)/shard_map/ppermute | solution.py:48
  15.6 1.5 collective-permute-done
  17.1 1.4 collective-permute-start.1
  18.5 2.6 collective-permute-done.1
  21.7 5.9 %collective-permute-done.2 = s32[4,5376]{1,0:T(4,128)S(1)} collective-permute-done((s32[4,5376]{1,0:T(4,128)S(1)}, s32[4,5376]{1,0:T(4,128)S(1)}, u32[]{:S(2)}, u32[]{:S(2)}) %collective-permute-start.2) | collective-permute-done | bytes 86048 | tf_op jit(solution)/shard_map/ppermute | solution.py:48
  27.9 1.8 ge.24
  29.8 2.8 reshape.57
  32.6 2.8 sub.36
  35.4 2.3 and_select_fusion
  37.7 7.9 %slice_reduce_fusion.9 = (s32[3072]{0:T(1024)S(1)}, s32[3072]{0:T(1024)S(1)}, s32[3072]{0:T(1024)S(1)}, s32[3072]{0:T(1024)S(1)}, s32[3072]{0:T(1024)S(1)}, /*in...) fusion(s32[3072,10]{1,0:T(8,128)S(1)} %and_select_fusion), kind=kLoop, calls=%fused_computation.40 | loop fusion | bytes 245760 | tf_op jit(solution)/shard_map/slice | solution.py:11
  45.6 19.4 %fusion.11 = bf16[3072,512]{1,0:T(8,128)(2,1)} fusion(s32[3072]{0:T(1024)S(1)} %get-tuple-element.6, s32[3072]{0:T(1024)S(1)} %get-tuple-element.7, s32[3072]{0:T(1024)S(1)} %get-tuple-element.8, s32[3072]{0:T(1024)S(1)} %get-tuple-element.9, s32[3072]{0:T(1024)S(1)} %get-tuple-element.10, s32[3072]{0:T(1024)S(1)} %get-tuple-element.11, ...), kind=kOutput, calls=%fused_computation.22 | convolution fusion | flops 3332227072 | bytes 4321280 | tf_op jit(solution)/shard_map/dot_general | solution.py:65
  65.7 3.6 %fusion.22 = f32[384,2048]{1,0:T(8,128)} fusion(bf16[512,2048]{1,0:T(8,128)(2,1)S(1)} %copy-done, bf16[1024,512]{1,0:T(8,128)(2,1)} %param.10), kind=kOutput, calls=%fused_computation.60 | convolution fusion | flops 805306368 | bytes 5636096 | tf_op jit(solution)/shard_map/dot_general | solution.py:70
  69.4 73.0 %reduce-scatter.4.cloned.1.call-done = bf16[384,512]{1,0:T(8,128)(2,1)} async-done(((bf16[3072,512]{1,0:T(8,128)(2,1)}), bf16[384,512]{1,0:T(8,128)(2,1)}) %reduce-scatter.4.cloned.1.call-update) | async-done | bytes 393232 | tf_op jit(solution)/shard_map/reduce_scatter | solution.py:66
  142.4 4.8 %add_convert_fusion.4 = bf16[384,2048]{1,0:T(8,128)(2,1)} fusion(f32[384,2048]{1,0:T(8,128)} %fusion.22, bf16[512,2048]{1,0:T(8,128)(2,1)} %param.13, bf16[384,512]{1,0:T(8,128)(2,1)} %reduce-scatter.4.cloned.1.call-done, f32[384]{0:T(512)S(1)} %convert_element_type.103), kind=kOutput, calls=%fused_computation.23 | convolution fusion | flops 807469056 | bytes 7210496 | tf_op jit(solution)/shard_map/dot_general | solution.py:71
  147.7 0.9 select_n.45
  148.6 2.5 slice_reduce_fusion.14
  151.1 23.4 %reduce-scatter.6.cloned.1.call-done = bf16[384,512]{1,0:T(8,128)(2,1)} async-done(((bf16[384,2048]{1,0:T(8,128)(2,1)}), bf16[384,512]{1,0:T(8,128)(2,1)}) %reduce-scatter.6.cloned.1.call-update) | async-done | bytes 393232 | tf_op jit(solution)/shard_map/reduce_scatter | solution.py:73
  174.6 1.0 broadcast_maximum_fusion
  175.6 4.7 %convolution_divide_fusion = f32[2048,256]{1,0:T(8,128)} fusion(s32[2048]{0:T(1024)S(1)} %get-tuple-element.16, s32[2048]{0:T(1024)S(1)} %get-tuple-element.17, s32[2048]{0:T(1024)S(1)} %get-tuple-element.18, s32[2048]{0:T(1024)S(1)} %get-tuple-element.19, s32[2048]{0:T(1024)S(1)} %get-tuple-element.15, bf16[512,256]{1,0:T(8,128)(2,1)S(1)} %copy-done.4, ...), kind=kOutput, calls=%fused_computation.30 | convolution fusion | flops 515932160 | bytes 2801664 | tf_op jit(solution)/shard_map/dot_general | solution.py:79
  180.3 1.9 fusion.17
  182.2 138.5 %reduce-scatter.8.cloned.1.call-done = f32[64,256]{1,0:T(8,128)} async-done(((f32[2048,256]{1,0:T(8,128)}), f32[64,256]{1,0:T(8,128)}) %reduce-scatter.8.cloned.1.call-update) | async-done | bytes 65552 | tf_op jit(solution)/shard_map/reduce_scatter | solution.py:84
  320.7 0.9 multiply_reduce_fusion
  321.7 1.5 multiply_convert_fusion
  (36 shorter events, 4.1 us)
Async XLA Ops:
  6.5 59.2 %copy-start = (bf16[512,2048]{1,0:T(8,128)(2,1)S(1)}, bf16[512,2048]{1,0:T(8,128)(2,1)}, u32[]{:S(2)}) copy-start(bf16[512,2048]{1,0:T(8,128)(2,1)} %param.12) | copy-start | bytes 6291460
  6.5 135.9 %reduce-scatter.4.cloned.1.call-start = ((), (), s32[]{:S(2)}) async-start(), calls=%async_computation.3 | async-start | bytes 3538944 | tf_op jit(solution)/shard_map/reduce_scatter | solution.py:66
  9.5 7.5 %collective-permute-start = (s32[1,5376]{1,0:T(1,128)S(1)}, s32[1,5376]{1,0:T(1,128)S(1)}, u32[]{:S(2)}, u32[]{:S(2)}) collective-permute-start(s32[1,5376]{1,0:T(1,128)S(1)} %reshape.55), channel_id=1, source_target_pairs={{0,28},{4,0},{8,4},{12,8},{16,12},{20,16},{24,20},{28,24},{1,29},{... | collective-permute-start | bytes 64520 | tf_op jit(solution)/shard_map/ppermute | solution.py:48
  17.1 4.1 %collective-permute-start.1 = (s32[2,5376]{1,0:T(2,128)S(1)}, s32[2,5376]{1,0:T(2,128)S(1)}, u32[]{:S(2)}, u32[]{:S(2)}) collective-permute-start(s32[2,5376]{1,0:T(2,128)S(1)} %pad_add_fusion.1), channel_id=1, source_target_pairs={{0,24},{4,28},{8,0},{12,4},{16,8},{20,12},{24,16},{28,20},{1,25},{... | collective-permute-start | bytes 129032 | tf_op jit(solution)/shard_map/ppermute | solution.py:48
  21.2 6.4 %collective-permute-start.2 = (s32[4,5376]{1,0:T(4,128)S(1)}, s32[4,5376]{1,0:T(4,128)S(1)}, u32[]{:S(2)}, u32[]{:S(2)}) collective-permute-start(s32[4,5376]{1,0:T(4,128)S(1)} %pad_add_fusion), channel_id=1, source_target_pairs={{0,16},{4,20},{8,24},{12,28},{16,0},{20,4},{24,8},{28,12},{1,17},{... | collective-permute-start | bytes 258056 | tf_op jit(solution)/shard_map/ppermute | solution.py:48
  37.7 7.9 %copy-start.2 = (bf16[1024,512]{1,0:T(8,128)(2,1)S(1)}, bf16[1024,512]{1,0:T(8,128)(2,1)}, u32[]{:S(2)}) copy-start(bf16[1024,512]{1,0:T(8,128)(2,1)} %param.10) | copy-start | bytes 3145732
  37.7 7.9 %copy-start.5 = (bf16[4,512]{1,0:T(4,128)(2,1)S(1)}, bf16[4,512]{1,0:T(4,128)(2,1)}, u32[]{:S(2)}) copy-start(bf16[4,512]{1,0:T(4,128)(2,1)} %param.11) | copy-start | bytes 12292
  65.0 0.7 copy-start.3
  65.1 109.5 %reduce-scatter.6.cloned.1.call-start = ((), (), s32[]{:S(2)}) async-start(), calls=%async_computation.4 | async-start | bytes 1966080 | tf_op jit(solution)/shard_map/reduce_scatter | solution.py:73
  147.3 173.5 %reduce-scatter.8.cloned.1.call-start = ((), (), s32[]{:S(2)}) async-start(), calls=%async_computation.5 | async-start | bytes 2162688 | tf_op jit(solution)/shard_map/reduce_scatter | solution.py:84
  148.6 27.0 %copy-start.4 = (bf16[512,256]{1,0:T(8,128)(2,1)S(1)}, bf16[512,256]{1,0:T(8,128)(2,1)}, u32[]{:S(2)}) copy-start(bf16[512,256]{1,0:T(8,128)(2,1)} %param.15) | copy-start | bytes 786436
  175.6 4.7 %copy-start.1 = (bf16[512,256]{1,0:T(8,128)(2,1)S(1)}, bf16[512,256]{1,0:T(8,128)(2,1)}, u32[]{:S(2)}) copy-start(bf16[512,256]{1,0:T(8,128)(2,1)} %param.14) | copy-start | bytes 786436
Sparse Core Ops, SparseCore 0:
  65.2 77.1 reduce-scatter.3
  147.4 27.1 reduce-scatter.5
  182.3 138.3 reduce-scatter.7
